TPU v7x, 32 devices: a whole 2x2x4 slice. The times are simulated.
32 devices in a mesh: dp: 2 (over y), hid: 4 (over x, core), wid: 4 (over z).
Axes of the slice: x: 2, y: 2, z: 4, core: 2. Of those that a mesh axis runs over, the one named last changes fastest.
Arguments:
- hidden_in: bfloat16 [6144, 1536], P('dp', 'wid'), may hold values from -6 to 6
- cotangent: bfloat16 [6144, 1536], P('dp', 'wid'), may hold values from -6 to 6
- segments: int32 [8, 768], P(('dp', 'wid')), may hold values from 0 to 2, never falling along the last dimension, each value on 1 to 512 neighbouring positions
- gain_attn: bfloat16 [1536], P(('dp', 'wid')), may hold values from 0.5 to 1.5
- gain_mlp: bfloat16 [1536], P(('dp', 'wid')), may hold values from 0.5 to 1.5
- in_weight: bfloat16 [1536, 4, 1536], P(('dp', 'wid'), None, 'hid'), may hold values from -0.15625 to 0.15625
- beta_weight: bfloat16 [1536, 12], P(('dp', 'wid'), 'hid'), may hold values from -0.15625 to 0.15625
- out_weight: bfloat16 [1536, 1536], P('hid', ('dp', 'wid')), may hold values from -2.5 to 2.5
- gate_weight: bfloat16 [1536, 4096], P(('dp', 'wid'), 'hid'), may hold values from -0.15625 to 0.15625
- up_weight: bfloat16 [1536, 4096], P(('dp', 'wid'), 'hid'), may hold values from -0.15625 to 0.15625
- down_weight: bfloat16 [4096, 1536], P('hid', ('dp', 'wid')), may hold values from -0.1875 to 0.1875
Outputs:
- output: bfloat16 [6144, 1536], P('dp', 'wid')
- grad_input: float32 [6144, 1536], P('dp', 'wid')
- grad_gain_attn: float32 [1536], P(('dp', 'wid'))
- grad_gain_mlp: float32 [1536], P(('dp', 'wid'))
- grad_in_weight: float32 [1536, 4, 1536], P(('dp', 'wid'), None, 'hid')
- grad_beta_weight: float32 [1536, 12], P(('dp', 'wid'), 'hid')
- grad_out_weight: float32 [1536, 1536], P('hid', ('dp', 'wid'))
- grad_gate_weight: float32 [1536, 4096], P(('dp', 'wid'), 'hid')
- grad_up_weight: float32 [1536, 4096], P(('dp', 'wid'), 'hid')
- grad_down_weight: float32 [4096, 1536], P('hid', ('dp', 'wid'))
Inputs may be any that keep to these rules, and one draw needn't show every extreme that they name: `segments`: in each row (the 768 tokens of one block) ids never fall, each of the 3 ids occurs in one run of 1 to 512 tokens, and one run is exactly 512 long.
All inputs are finite; a program needn't handle non-finite values.
Results may differ from a plain program's by a relative error of at most 0.012.
The roundings to bfloat16 on the way count: a program that leaves them out, or rounds other values in their place, can miss the bound.
Values may be sent and summed in bfloat16 or wider, within the bound.
No kernel may reach another device: no remote copies, remote signals or barrier semaphores. Data moves between devices by JAX's collectives and lax.ppermute only.
A program may use at most 256 MiB of HBM per device.

v0:
```python
import jax
import jax.numpy as jnp
from jax import lax
from jax.sharding import PartitionSpec as P

HD = 128
BLK = 64


def householder_attention(
    queries, key_vecs, value_vecs, raw_dirs, beta_logit, segment_ids, block_size
):
    highest = lax.Precision.HIGHEST
    length, head_count, head_width = queries.shape
    block_count = length // block_size
    directions = raw_dirs * lax.rsqrt(jnp.sum(raw_dirs * raw_dirs, axis=-1, keepdims=True) + 1e-06)
    strengths = 2.0 * jax.nn.sigmoid(beta_logit)
    query_blocks = queries.reshape(block_count, block_size, head_count, head_width)
    key_blocks = key_vecs.reshape(block_count, block_size, head_count, head_width)
    dir_blocks = directions.reshape(block_count, block_size, head_count, head_width)
    strength_blocks = strengths.reshape(block_count, block_size, head_count).transpose(0, 2, 1)
    offsets = jnp.arange(block_size)
    strict_lower = (offsets[:, None] > offsets[None, :]).astype(jnp.float32)
    lower_incl = (offsets[:, None] >= offsets[None, :]).astype(jnp.float32)
    identity = jnp.eye(block_size, dtype=jnp.float32)
    gram_matrix = jnp.einsum("nshd,nthd->nhst", dir_blocks, dir_blocks, precision=highest)
    system = identity + strength_blocks[..., :, None] * gram_matrix * strict_lower
    right_side = identity * strength_blocks[..., :, None]
    tri_factor = jax.scipy.linalg.solve_triangular(
        system, right_side, lower=True, unit_diagonal=True
    )
    query_dirs = (
        jnp.einsum("nihd,nshd->nhis", query_blocks, dir_blocks, precision=highest) * lower_incl
    )
    dir_keys = (
        jnp.einsum("nthd,njhd->nhtj", dir_blocks, key_blocks, precision=highest) * strict_lower
    )
    factor_keys = jnp.einsum("nhst,nhtj->nhsj", tri_factor, dir_keys, precision=highest)
    inner_scores = jnp.einsum("nihd,njhd->nhij", query_blocks, key_blocks, precision=highest)
    inner_scores = inner_scores - jnp.einsum(
        "nhis,nhsj->nhij", query_dirs, factor_keys, precision=highest
    )
    keys_moved = key_blocks - jnp.einsum(
        "nhsj,nshd->njhd", factor_keys, dir_blocks, precision=highest
    )
    query_factor = jnp.einsum("nhis,nhst->nhit", query_dirs, tri_factor, precision=highest)
    queries_moved = query_blocks - jnp.einsum(
        "nhit,nthd->nihd", query_factor, dir_blocks, precision=highest
    )

    def sweep_step(moved_rows, item):
        block_index, keys_here, dirs_here, factor_here, inner_here, queries_here = item
        start = block_index * block_size
        zero_index = start * 0
        scores = jnp.einsum("ihd,jhd->hij", moved_rows, keys_here, precision=highest)
        scores = lax.dynamic_update_slice(scores, inner_here, (zero_index, start, zero_index))
        projected = jnp.einsum("ihd,shd->his", moved_rows, dirs_here, precision=highest)
        projected = jnp.einsum("his,hst->hit", projected, factor_here, precision=highest)
        moved_rows = moved_rows - jnp.einsum(
            "hit,thd->ihd", projected, dirs_here, precision=highest
        )
        moved_rows = lax.dynamic_update_slice(
            moved_rows, queries_here, (start, zero_index, zero_index)
        )
        return (moved_rows, scores)

    initial = jnp.zeros((length, head_count, head_width), jnp.float32)
    items = (
        jnp.arange(block_count, dtype=jnp.int32),
        keys_moved,
        dir_blocks,
        tri_factor,
        inner_scores,
        queries_moved,
    )
    _, scores = lax.scan(jax.checkpoint(sweep_step), initial, items, reverse=True)
    scores = scores.transpose(1, 2, 0, 3).reshape(head_count, length, length)
    position = jnp.arange(length)
    allowed = (position[None, :] <= position[:, None]) & (
        segment_ids[:, None] == segment_ids[None, :]
    )
    scores = jnp.where(allowed[None], scores * head_width ** (-0.5), -1e30)
    row_top = jnp.max(scores, axis=-1, keepdims=True)
    exponent = jnp.exp(scores - row_top)
    attn_probs = exponent / jnp.sum(exponent, axis=-1, keepdims=True)
    return jnp.einsum("hij,jhd->ihd", attn_probs, value_vecs, precision=highest)


def norm_back(values, scale_row, gain, grad_out):
    weighted = grad_out * gain
    grad_gain = jnp.sum(grad_out * values * scale_row, axis=0)
    grad_values = scale_row * weighted - values * scale_row**3 * jnp.mean(
        weighted * values, axis=-1, keepdims=True
    )
    return (grad_gain, grad_values)


def body(
    hidden_in,
    cotangent,
    segments,
    gain_attn,
    gain_mlp,
    in_weight,
    beta_weight,
    out_weight,
    gate_weight,
    up_weight,
    down_weight,
):
    highest = lax.Precision.HIGHEST
    token_in, token_grad = (
        lax.all_to_all(hidden_in, "wid", split_axis=0, concat_axis=1, tiled=True),
        lax.all_to_all(cotangent, "wid", split_axis=0, concat_axis=1, tiled=True),
    )
    gathered = (
        lax.all_gather(gain_attn, ("dp", "wid"), axis=0, tiled=True),
        lax.all_gather(gain_mlp, ("dp", "wid"), axis=0, tiled=True),
        lax.all_gather(in_weight, ("dp", "wid"), axis=0, tiled=True),
        lax.all_gather(beta_weight, ("dp", "wid"), axis=0, tiled=True),
        lax.all_gather(out_weight, ("dp", "wid"), axis=1, tiled=True),
        lax.all_gather(gate_weight, ("dp", "wid"), axis=0, tiled=True),
        lax.all_gather(up_weight, ("dp", "wid"), axis=0, tiled=True),
        lax.all_gather(down_weight, ("dp", "wid"), axis=1, tiled=True),
    )
    gain_one, gain_two, weight_in, weight_beta, weight_out, weight_gate, weight_up, weight_down = (
        gathered
    )
    gain_one = gain_one.astype(jnp.float32)
    gain_two = gain_two.astype(jnp.float32)
    row_count = token_in.shape[0]
    head_count = weight_beta.shape[1]
    seg_row = segments[0]
    inputs = token_in.astype(jnp.float32)
    scale_one = lax.rsqrt(jnp.mean(inputs * inputs, axis=-1, keepdims=True) + 1e-06)
    normed = (inputs * scale_one * gain_one).astype(jnp.bfloat16)
    projected = jnp.einsum(
        "td,dkc->tkc", normed, weight_in, preferred_element_type=jnp.float32
    ).astype(jnp.bfloat16)
    logits = jnp.dot(normed, weight_beta, preferred_element_type=jnp.float32)
    pieces = projected.astype(jnp.float32).reshape(row_count, 4, head_count, HD)
    query_in = pieces[:, 0]
    key_in = pieces[:, 1]
    value_in = pieces[:, 2]
    dirs_in = pieces[:, 3]

    def attend(queries, key_vecs, value_vecs, raw_dirs, beta_logit):
        return householder_attention(
            queries, key_vecs, value_vecs, raw_dirs, beta_logit, seg_row, BLK
        )

    attended = attend(query_in, key_in, value_in, dirs_in, logits)
    attended = attended.reshape(row_count, head_count * HD).astype(jnp.bfloat16)
    branch = lax.psum(jnp.dot(attended, weight_out, preferred_element_type=jnp.float32), "hid")
    middle = inputs + branch
    scale_two = lax.rsqrt(jnp.mean(middle * middle, axis=-1, keepdims=True) + 1e-06)
    mixed = (middle * scale_two * gain_two).astype(jnp.bfloat16)
    gate = jnp.dot(mixed, weight_gate, preferred_element_type=jnp.float32)
    upward = jnp.dot(mixed, weight_up, preferred_element_type=jnp.float32)
    sigmoid_gate = jax.nn.sigmoid(gate)
    silu_gate = gate * sigmoid_gate
    product = (silu_gate * upward).astype(jnp.bfloat16)
    feed = lax.psum(
        jnp.dot(product, weight_down, preferred_element_type=jnp.float32).astype(jnp.bfloat16),
        "hid",
    ).astype(jnp.float32)
    output = lax.all_to_all(
        (middle + feed).astype(jnp.bfloat16), "wid", split_axis=1, concat_axis=0, tiled=True
    )
    grad_product = jnp.einsum(
        "td,fd->tf", token_grad, weight_down, preferred_element_type=jnp.float32
    )
    grad_down = jnp.einsum("tf,td->fd", product, token_grad, preferred_element_type=jnp.float32)
    grad_gate_pre = (
        grad_product * upward * sigmoid_gate * (1.0 + gate * (1.0 - sigmoid_gate))
    ).astype(jnp.bfloat16)
    grad_up_pre = (grad_product * silu_gate).astype(jnp.bfloat16)
    grad_mixed_part = jnp.einsum(
        "tf,df->td", grad_gate_pre, weight_gate, preferred_element_type=jnp.float32
    )
    grad_mixed_part = grad_mixed_part + jnp.einsum(
        "tf,df->td", grad_up_pre, weight_up, preferred_element_type=jnp.float32
    )
    grad_gate = jnp.einsum("td,tf->df", mixed, grad_gate_pre, preferred_element_type=jnp.float32)
    grad_up = jnp.einsum("td,tf->df", mixed, grad_up_pre, preferred_element_type=jnp.float32)
    grad_mixed = lax.psum(grad_mixed_part, "hid")
    grad_gain_two, grad_middle = norm_back(middle, scale_two, gain_two, grad_mixed)
    grad_middle = grad_middle + token_grad.astype(jnp.float32)
    grad_branch = grad_middle.astype(jnp.bfloat16)
    grad_attended = jnp.einsum(
        "td,cd->tc", grad_branch, weight_out, preferred_element_type=jnp.float32
    )
    grad_out = jnp.einsum("tc,td->cd", attended, grad_branch, preferred_element_type=jnp.float32)
    grad_heads = grad_attended.reshape(row_count, head_count, HD)
    _, attend_again = jax.vjp(attend, query_in, key_in, value_in, dirs_in, logits)
    grads_attn = attend_again(grad_heads)
    grad_query, grad_key, grad_value, grad_dirs, grad_logit = grads_attn
    grad_proj = jnp.stack((grad_query, grad_key, grad_value, grad_dirs), axis=1)
    grad_proj = grad_proj.reshape(row_count, 4, head_count * HD).astype(jnp.bfloat16)
    grad_normed_part = jnp.einsum(
        "tkc,dkc->td", grad_proj, weight_in, preferred_element_type=jnp.float32
    )
    grad_normed_part = grad_normed_part + jnp.dot(
        grad_logit, weight_beta.astype(jnp.float32).T, precision=highest
    )
    grad_in = jnp.einsum("td,tkc->dkc", normed, grad_proj, preferred_element_type=jnp.float32)
    grad_beta = jnp.dot(normed.astype(jnp.float32).T, grad_logit, precision=highest)
    grad_normed = lax.psum(grad_normed_part, "hid")
    grad_gain_one, grad_inputs = norm_back(inputs, scale_one, gain_one, grad_normed)
    grad_inputs = grad_inputs + grad_middle
    grad_input = lax.all_to_all(grad_inputs, "wid", split_axis=1, concat_axis=0, tiled=True)
    shares = (
        lax.psum_scatter(grad_gain_one, ("dp", "wid"), scatter_dimension=0, tiled=True),
        lax.psum_scatter(grad_gain_two, ("dp", "wid"), scatter_dimension=0, tiled=True),
        lax.psum_scatter(grad_in, ("dp", "wid"), scatter_dimension=0, tiled=True),
        lax.psum_scatter(grad_beta, ("dp", "wid"), scatter_dimension=0, tiled=True),
        lax.psum_scatter(grad_out, ("dp", "wid"), scatter_dimension=1, tiled=True),
        lax.psum_scatter(grad_gate, ("dp", "wid"), scatter_dimension=0, tiled=True),
        lax.psum_scatter(grad_up, ("dp", "wid"), scatter_dimension=0, tiled=True),
        lax.psum_scatter(grad_down, ("dp", "wid"), scatter_dimension=1, tiled=True),
    )
    return (
        output,
        grad_input,
        shares[0],
        shares[1],
        shares[2],
        shares[3],
        shares[4],
        shares[5],
        shares[6],
        shares[7],
    )


def solution(mesh):
    placed = (
        P("dp", "wid"),
        P("dp", "wid"),
        P(("dp", "wid"), None),
        P(("dp", "wid")),
        P(("dp", "wid")),
        P(("dp", "wid"), None, "hid"),
        P(("dp", "wid"), "hid"),
        P("hid", ("dp", "wid")),
        P(("dp", "wid"), "hid"),
        P(("dp", "wid"), "hid"),
        P("hid", ("dp", "wid")),
    )
    return jax.shard_map(
        body,
        mesh=mesh,
        in_specs=placed,
        out_specs=(
            P("dp", "wid"),
            P("dp", "wid"),
            P(("dp", "wid")),
            P(("dp", "wid")),
            P(("dp", "wid"), None, "hid"),
            P(("dp", "wid"), "hid"),
            P("hid", ("dp", "wid")),
            P(("dp", "wid"), "hid"),
            P(("dp", "wid"), "hid"),
            P("hid", ("dp", "wid")),
        ),
        check_vma=False,
    )
```

profile of v0, /device:TPU:0, one launch (start us, length us, event | category | flops | bytes accessed | tf_op | source)
XLA Modules:
  0.0 2532.5 jit_solution(9748514839555380016)
XLA Ops:
  9.3 6.5 all-to-all-start
  18.4 89.2 %all-reduce.5 = (bf16[1536]{0:T(1024)(128)(2,1)S(1)}, bf16[1536]{0:T(1024)(128)(2,1)S(1)}) all-reduce(bf16[1536]{0:T(1024)(128)(2,1)S(1)} %dynamic-update-slice, bf16[1536]{0:T(1024)(128)(2,1)S(1)} %dynamic-update-slice.1), channel_id=1, replica_groups=mesh['dp'=2,'hid'=4,'wid'=4] {'dp','wid'}, use_global_device_ids=true, to_apply=%add | all-reduce | flops 3072 | bytes 12288
  107.6 27.1 %all-gather = bf16[8,192,3]{1,2,0:T(4,128)(2,1)S(1)} all-gather(bf16[1,192,3]{1,2,0:T(4,128)(2,1)S(1)} %bitcast.620), channel_id=1, replica_groups=mesh['dp'=2,'hid'=4,'wid'=4] {'dp','wid'}, dimensions={0}, use_global_device_ids=true | all-gather | bytes 10368 | tf_op jit(solution)/shard_map/all_gather | solution.py:120
  142.9 6.2 fusion.66
  158.4 177.1 %custom-call.8 = f32[12,3,1,64,64]{3,4,2,1,0:T(8,128)S(1)} custom-call(f32[12,3,1,64,64]{4,3,2,1,0:T(8,128)S(1)} %add_bitcast_fusion), custom_call_target="InvertDiagBlocksLowerTriangular" | custom-call | tf_op jit(solution)/shard_map/jit(_solve_triangular)/vmap(vmap())/triangular_solve/custom-call.1 | solution.py:29
  360.9 4.6 fusion.82
  372.6 6.7 broadcast_in_dim.127
  379.3 3.7 broadcast.244.clone.1
  383.1 167.9 %while.59 = (s32[]{:T(128)}, f32[768,3,128]{0,2,1:T(8,128)S(1)}, f32[12,3,768,64]{2,3,1,0:T(8,128)}, f32[12,768,3,128]{1,3,2,0:T(8,128)}, f32[12,64,3,128]{3,1,2...) while((s32[]{:T(128)}, f32[768,3,128]{0,2,1:T(8,128)S(1)}, ...), condition=%wide.region_12.14_spmd.clone, body=%wide.region_11.13_spmd.sunk.clone | while | flops 793018368 | bytes 12189915 | solution.py:76
  551.0 3.7 broadcast.244.clone
  554.8 155.0 %while.58 = (s32[]{:T(128)}, f32[768,3,128]{0,2,1:T(8,128)S(1)}, f32[12,3,768,64]{2,3,1,0:T(8,128)}, f32[12,64,3,128]{3,1,2,0:T(8,128)}, f32[12,3,64,64]{2,3,1,0...) while((s32[]{:T(128)}, f32[768,3,128]{0,2,1:T(8,128)S(1)}, ...), condition=%wide.region_3.5_spmd.clone, body=%wide.region_2.4_spmd.sunk.clone | while | flops 793018368 | bytes 9830607 | solution.py:76
  709.8 6.3 select_reduce_fusion.1
  719.0 3.9 exponential_reduce_fusion
  726.2 3.7 convolution_convert_fusion.1
  730.0 5.0 fusion.167
  736.2 3.8 all-to-all-start.2
  740.7 39.9 %all-to-all-done.2 = bf16[4,768,384]{2,1,0:T(8,128)(2,1)S(1)} async-done(((bf16[4,768,384]{2,1,0:T(8,128)(2,1)}), bf16[4,768,384]{2,1,0:T(8,128)(2,1)S(1)}, u32[]{:S(2)}, u32[]{:S(2)}) %all-to-all-start.2) | async-done | bytes 2359328 | tf_op jit(solution)/shard_map/all_to_all | solution.py:114
  783.9 43.4 %all-reduce.11.cloned.1.call-done = f32[768,1536]{1,0:T(8,128)} async-done(((f32[768,1536]{1,0:T(8,128)}), f32[768,1536]{1,0:T(8,128)}) %all-reduce.11.cloned.1.call-update) | async-done | bytes 4718608 | tf_op jit(solution)/shard_map/psum | solution.py:154
  827.3 4.4 multiply_reduce_fusion.5
  835.7 54.2 %all-gather.11.cloned.1.call-done = bf16[1536,1024]{1,0:T(8,128)(2,1)} async-done(((bf16[192,1024]{1,0:T(8,128)(2,1)}), bf16[1536,1024]{1,0:T(8,128)(2,1)}) %all-gather.11.cloned.1.call-update) | async-done | bytes 3145744 | tf_op jit(solution)/shard_map/all_gather | solution.py:122
  889.9 6.9 fusion.168
  896.8 54.2 %all-gather.13.cloned.1.call-done = bf16[1536,1024]{1,0:T(8,128)(2,1)} async-done(((bf16[192,1024]{1,0:T(8,128)(2,1)}), bf16[1536,1024]{1,0:T(8,128)(2,1)}) %all-gather.13.cloned.1.call-update) | async-done | bytes 3145744 | tf_op jit(solution)/shard_map/all_gather | solution.py:123
  951.0 6.8 fusion.169
  957.8 54.2 %all-gather.15.cloned.1.call-done = bf16[1024,1536]{0,1:T(8,128)(2,1)} async-done(((bf16[1024,192]{0,1:T(8,128)(2,1)}), bf16[1024,1536]{0,1:T(8,128)(2,1)}) %all-gather.15.cloned.1.call-update) | async-done | bytes 3145744 | tf_op jit(solution)/shard_map/all_gather | solution.py:124
  1012.0 7.9 multiply_convert_fusion.2
  1023.0 4.5 convolution_add_fusion
  1028.8 5.7 convolution_convert_fusion
  1034.6 3.6 multiply_bitcast_fusion
  1041.6 78.6 %all-reduce.15.cloned.1.call-done = f32[768,1536]{1,0:T(8,128)} async-done(((f32[768,1536]{1,0:T(8,128)}), f32[768,1536]{1,0:T(8,128)}) %all-reduce.15.cloned.1.call-update) | async-done | bytes 4718608 | tf_op jit(solution)/shard_map/psum | solution.py:186
  1120.2 5.7 multiply_reduce_fusion.1
  1125.9 52.5 %all-reduce.13.cloned.1.call-done = bf16[768,1536]{1,0:T(8,128)(2,1)} async-done(((bf16[768,1536]{1,0:T(8,128)(2,1)}), bf16[768,1536]{1,0:T(8,128)(2,1)}) %all-reduce.13.cloned.1.call-update) | async-done | bytes 2359312 | tf_op jit(solution)/shard_map/psum | solution.py:163
  1178.4 7.9 convert_add_fusion
  1188.4 9.1 subtract_exponential_fusion
  1200.1 3.5 select_multiply_fusion
  1203.6 3.6 copy.345
  1207.2 388.8 %while.60 = (s32[]{:T(128)}, f32[768,3,128]{2,0,1:T(8,128)}, f32[12,64,3,128]{3,1,2,0:T(8,128)}, f32[12,64,3,128]{3,1,2,0:T(8,128)}, f32[12,3,64,64]{3,2,1,0:T(8...) while((s32[]{:T(128)}, f32[768,3,128]{2,0,1:T(8,128)}, ...), condition=%wide.region_19.21_spmd.clone.clone, body=%wide.region_18.20_spmd.clone.sunk.clone | while | flops 1926684672 | bytes 39472068 | solution.py:76
  1603.5 3.4 convolution_add_fusion.3
  1610.2 3.5 convolution_add_fusion.2
  1621.0 3.5 convolution_bitcast_fusion.14
  1629.1 3.5 fusion.75
  1641.0 3.4 convolution_bitcast_fusion.17
  1650.8 10.9 fusion.86
  1664.0 3.8 fusion.81
  1677.7 5.9 fusion.125
  1683.6 4.5 bitcast_add_fusion
  1689.8 4.1 fusion.140
  1694.0 7.7 fusion.60
  1702.8 5.3 fusion.103
  1709.8 6.0 fusion.173
  1715.8 6.2 fusion.174
  1723.7 6.0 fusion.175
  1733.0 4.8 all-to-all-start.1
  1737.8 44.6 %all-reduce.17.cloned.1.call-done = f32[768,1536]{1,0:T(8,128)} async-done(((f32[768,1536]{1,0:T(8,128)}), f32[768,1536]{1,0:T(8,128)}) %all-reduce.17.cloned.1.call-update) | async-done | bytes 4718608 | tf_op jit(solution)/shard_map/psum | solution.py:208
  1782.4 5.1 multiply_reduce_fusion.2
  1787.5 4.5 subtract_add_fusion
  1794.5 5.1 all-to-all-start.3
  1800.2 116.1 %reduce-scatter.19.cloned.1.call-done = f32[192,3]{1,0:T(8,128)} async-done(((f32[1536,3]{1,0:T(8,128)}), f32[192,3]{1,0:T(8,128)}) %reduce-scatter.19.cloned.1.call-update) | async-done | bytes 2320
  1917.9 36.1 %all-reduce.4 = (f32[1536]{0:T(1024)S(1)}, f32[1536]{0:T(1024)S(1)}) all-reduce(f32[1536]{0:T(1024)S(1)} %get-tuple-element.653, f32[1536]{0:T(1024)S(1)} %copy-done.83), channel_id=2, replica_groups=mesh['dp'=2,'hid'=4,'wid'=4] {'dp','wid'}, use_global_device_ids=true, to_apply=%region_26.29.clone | all-reduce | flops 3072 | bytes 24576
  1955.3 127.3 %reduce-scatter.9.cloned.1.call-done = f32[192,4,384]{2,0,1:T(8,128)} async-done(((f32[1536,4,384]{2,0,1:T(8,128)}), f32[192,4,384]{2,0,1:T(8,128)}) %reduce-scatter.9.cloned.1.call-update) | async-done | bytes 1179664 | tf_op jit(solution)/shard_map/reduce_scatter | solution.py:215
  2085.6 69.3 %reduce-scatter.11.cloned.1.call-done = f32[384,192]{0,1:T(8,128)} async-done(((f32[384,1536]{0,1:T(8,128)}), f32[384,192]{0,1:T(8,128)}) %reduce-scatter.11.cloned.1.call-update) | async-done | bytes 294928 | tf_op jit(solution)/shard_map/reduce_scatter | solution.py:217
  2154.9 121.6 %reduce-scatter.13.cloned.1.call-done = f32[192,1024]{1,0:T(8,128)} async-done(((f32[1536,1024]{1,0:T(8,128)}), f32[192,1024]{1,0:T(8,128)}) %reduce-scatter.13.cloned.1.call-update) | async-done | bytes 786448 | tf_op jit(solution)/shard_map/reduce_scatter | solution.py:218
  2276.5 121.5 %reduce-scatter.15.cloned.1.call-done = f32[192,1024]{1,0:T(8,128)} async-done(((f32[1536,1024]{1,0:T(8,128)}), f32[192,1024]{1,0:T(8,128)}) %reduce-scatter.15.cloned.1.call-update) | async-done | bytes 786448 | tf_op jit(solution)/shard_map/reduce_scatter | solution.py:219
  2398.0 121.6 %reduce-scatter.17.cloned.1.call-done = f32[1024,192]{0,1:T(8,128)} async-done(((f32[1024,1536]{0,1:T(8,128)}), f32[1024,192]{0,1:T(8,128)}) %reduce-scatter.17.cloned.1.call-update) | async-done | bytes 786448 | tf_op jit(solution)/shard_map/reduce_scatter | solution.py:220
  2521.0 4.8 copy.419
  (1043 shorter events, 834.2 us)
Async XLA Ops:
  7.2 135.7 %all-gather.7.cloned.1.call-start = ((), (), s32[]{:S(2)}) async-start(), calls=%async_computation.10 | async-start | bytes 5308416 | tf_op jit(solution)/shard_map/all_gather | solution.py:119
  9.2 7.3 copy-start.87
  9.2 8.6 copy-start.90
  9.2 8.9 copy-start.91
  9.2 98.3 %copy-start.86 = (bf16[192,3]{0,1:T(4,128)(2,1)S(1)}, bf16[192,3]{0,1:T(4,128)(2,1)}, u32[]{:S(2)}) copy-start(bf16[192,3]{0,1:T(4,128)(2,1)} %param.27) | copy-start | bytes 3460
  9.2 125.5 %copy-start.85 = (s32[1,768]{1,0:T(1,128)S(1)}, s32[1,768]{1,0:T(1,128)}, u32[]{:S(2)}) copy-start(s32[1,768]{1,0:T(1,128)} %param.23) | copy-start | bytes 9220
  9.3 128.9 %all-to-all-start = ((bf16[4,768,384]{2,1,0:T(8,128)(2,1)}), bf16[4,768,384]{2,1,0:T(8,128)(2,1)S(1)}, u32[]{:S(2)}, u32[]{:S(2)}) async-start(bf16[4,768,384]{2,1,0:T(8,128)(2,1)} %bitcast.612), calls=%async_computation | async-start | bytes 4718592 | tf_op jit(solution)/shard_map/all_to_all | solution.py:113
  15.7 714.3 %all-gather.9.cloned.1.call-start = ((), (), s32[]{:S(2)}) async-start(), calls=%async_computation.11 | async-start | bytes 1327104 | tf_op jit(solution)/shard_map/all_gather | solution.py:121
  16.5 810.9 %all-reduce.11.cloned.1.call-start = ((), (), s32[]{:S(2)}) async-start(), calls=%async_computation.12 | async-start | bytes 9437184 | tf_op jit(solution)/shard_map/psum | solution.py:154
  107.6 33.2 %copy-start.69 = (f32[1536]{0:T(1024)}, f32[1536]{0:T(1024)S(1)}, u32[]{:S(2)}) copy-start(f32[1536]{0:T(1024)S(1)} %convert_element_type.109) | copy-start | bytes 18436
  134.8 6.4 copy-start.72
  135.5 22.3 copy-start.58
  135.6 22.2 copy-start.65
  135.6 22.2 copy-start.79
  142.9 14.9 copy-start.61
  154.7 213.6 %copy-start = (f32[12,64,3,128]{3,1,0,2:T(8,128)}, f32[12,64,3,128]{3,1,0,2:T(8,128)S(1)}, u32[]{:S(2)}) copy-start(f32[12,64,3,128]{3,1,0,2:T(8,128)S(1)} %broadcast_multiply_fusion) | copy-start | bytes 3538948
  338.7 13.2 copy-start.10
  346.6 14.3 copy-start.14
  554.8 155.0 %copy-start.50 = (pred[768,12,64]{0,2,1:T(8,128)(4,1)S(1)}, pred[768,12,64]{0,2,1:T(8,128)(4,1)}, u32[]{:S(2)}) copy-start(pred[768,12,64]{0,2,1:T(8,128)(4,1)} %fusion.65) | copy-start | bytes 1769476
  709.8 6.4 slice-start.2
  709.8 7.2 slice-start.3
  709.8 9.2 copy-start.7
  730.0 5.1 copy-start.48
  735.1 154.8 %all-gather.11.cloned.1.call-start = ((), (), s32[]{:S(2)}) async-start(), calls=%async_computation.13 | async-start | bytes 3538944 | tf_op jit(solution)/shard_map/all_gather | solution.py:122
  735.7 215.3 %all-gather.13.cloned.1.call-start = ((), (), s32[]{:S(2)}) async-start(), calls=%async_computation.14 | async-start | bytes 3538944 | tf_op jit(solution)/shard_map/all_gather | solution.py:123
  736.2 44.3 %all-to-all-start.2 = ((bf16[4,768,384]{2,1,0:T(8,128)(2,1)}), bf16[4,768,384]{2,1,0:T(8,128)(2,1)S(1)}, u32[]{:S(2)}, u32[]{:S(2)}) async-start(bf16[4,768,384]{2,1,0:T(8,128)(2,1)} %bitcast.613), calls=%async_computation.2 | async-start | bytes 4718592 | tf_op jit(solution)/shard_map/all_to_all | solution.py:114
  740.0 272.0 %all-gather.15.cloned.1.call-start = ((), (), s32[]{:S(2)}) async-start(), calls=%async_computation.15 | async-start | bytes 3538944 | tf_op jit(solution)/shard_map/all_gather | solution.py:124
  740.6 379.6 %all-reduce.15.cloned.1.call-start = ((), (), s32[]{:S(2)}) async-start(), calls=%async_computation.17 | async-start | bytes 9437184 | tf_op jit(solution)/shard_map/psum | solution.py:186
  783.9 228.1 %copy-start.44 = (bf16[4,96,8,384]{3,2,0,1:T(8,128)(2,1)}, bf16[4,96,8,384]{3,2,0,1:T(8,128)(2,1)S(1)}, u32[]{:S(2)}) copy-start(bf16[4,96,8,384]{3,2,0,1:T(8,128)(2,1)S(1)} %copy.300) | copy-start | bytes 7077892
  1012.0 7.9 copy-start.88
  1027.4 151.0 %all-reduce.13.cloned.1.call-start = ((), (), s32[]{:S(2)}) async-start(), calls=%async_computation.16 | async-start | bytes 4718592 | tf_op jit(solution)/shard_map/psum | solution.py:163
  1034.6 747.8 %all-reduce.17.cloned.1.call-start = ((), (), s32[]{:S(2)}) async-start(), calls=%async_computation.18 | async-start | bytes 9437184 | tf_op jit(solution)/shard_map/psum | solution.py:208
  1120.2 68.2 %slice-start = ((s8[7077888]{0:T(1024)(128)(4,1)}), s8[2883584]{0:T(1024)(128)(4,1)S(1)}, s32[]{:S(2)}) async-start(s8[7077888]{0:T(1024)(128)(4,1)} %bitcast.575), calls=%async_computation.25 | async-start | bytes 5767168
  1178.4 7.9 copy-start.56
  1178.4 10.0 slice-start.1
  1188.4 9.1 copy-start.51
  1207.2 388.9 %copy-start.1 = (f32[12,64,3,128]{3,1,0,2:T(8,128)S(1)}, f32[12,64,3,128]{3,1,0,2:T(8,128)}, u32[]{:S(2)}) copy-start(f32[12,64,3,128]{3,1,0,2:T(8,128)} %copy-done) | copy-start | bytes 3538948
  1219.3 3.7 copy-start.19
  1251.6 3.7 copy-start.19
  1284.2 3.7 copy-start.19
  1316.4 3.7 copy-start.19
  1381.3 3.7 copy-start.19
  1413.9 3.7 copy-start.19
  1478.9 3.6 copy-start.19
  1543.7 3.7 copy-start.19
  1575.9 3.7 copy-start.19
  1646.6 4.2 copy-start.52
  1664.0 3.8 copy-start.41
  1677.7 5.9 copy-start.74
  1677.7 5.9 copy-start.71
  1677.7 5.9 copy-start.73
  1688.1 228.2 %reduce-scatter.19.cloned.1.call-start = ((), (), s32[]{:S(2)}) async-start(), calls=%async_computation.24 | async-start | bytes 884736
  1693.9 388.6 %reduce-scatter.9.cloned.1.call-start = ((), (), s32[]{:S(2)}) async-start(), calls=%async_computation.19 | async-start | bytes 10616832 | tf_op jit(solution)/shard_map/reduce_scatter | solution.py:215
  1701.8 453.2 %reduce-scatter.11.cloned.1.call-start = ((), (), s32[]{:S(2)}) async-start(), calls=%async_computation.20 | async-start | bytes 2654208 | tf_op jit(solution)/shard_map/reduce_scatter | solution.py:217
  1708.1 568.4 %reduce-scatter.13.cloned.1.call-start = ((), (), s32[]{:S(2)}) async-start(), calls=%async_computation.21 | async-start | bytes 7077888 | tf_op jit(solution)/shard_map/reduce_scatter | solution.py:218
  1715.8 682.2 %reduce-scatter.15.cloned.1.call-start = ((), (), s32[]{:S(2)}) async-start(), calls=%async_computation.22 | async-start | bytes 7077888 | tf_op jit(solution)/shard_map/reduce_scatter | solution.py:219
  1722.1 797.5 %reduce-scatter.17.cloned.1.call-start = ((), (), s32[]{:S(2)}) async-start(), calls=%async_computation.23 | async-start | bytes 7077888 | tf_op jit(solution)/shard_map/reduce_scatter | solution.py:220
  1733.0 49.4 %copy-start.70 = (f32[1536]{0:T(1024)S(1)}, f32[1536]{0:T(1024)}, u32[]{:S(2)}) copy-start(f32[1536]{0:T(1024)} %copy-done.69) | copy-start | bytes 18436
  1733.0 49.4 %copy-start.82 = (f32[768]{0:T(1024)S(1)}, f32[768]{0:T(1024)}, u32[]{:S(2)}) copy-start(f32[768]{0:T(1024)} %copy-done.81) | copy-start | bytes 9220
  1733.0 61.5 %all-to-all-start.1 = ((bf16[768,4,384]{2,0,1:T(8,128)(2,1)}), bf16[768,4,384]{2,0,1:T(8,128)(2,1)S(1)}, u32[]{:S(2)}, u32[]{:S(2)}) async-start(bf16[768,4,384]{2,0,1:T(8,128)(2,1)} %bitcast.603), calls=%async_computation.1 | async-start | bytes 4718592 | tf_op jit(solution)/shard_map/all_to_all | solution.py:167
  1737.8 49.7 %copy-start.84 = (f32[768]{0:T(1024)S(1)}, f32[768]{0:T(1024)}, u32[]{:S(2)}) copy-start(f32[768]{0:T(1024)} %get-tuple-element.744) | copy-start | bytes 9220
  1782.4 5.1 copy-start.22
  1794.5 123.4 %copy-start.83 = (f32[1536]{0:T(1024)S(1)}, f32[1536]{0:T(1024)}, u32[]{:S(2)}) copy-start(f32[1536]{0:T(1024)} %get-tuple-element.651) | copy-start | bytes 18436
  1794.5 160.8 %all-to-all-start.3 = ((f32[768,4,384]{2,0,1:T(8,128)}), f32[768,4,384]{2,0,1:T(8,128)}, u32[]{:S(2)}, u32[]{:S(2)}) async-start(f32[768,4,384]{2,0,1:T(8,128)} %bitcast.585), calls=%async_computation.3 | async-start | bytes 9437184 | tf_op jit(solution)/shard_map/all_to_all | solution.py:211
  (142 other events, 295.5 us)
Sparse Core Ops, SparseCore 0:
  10.7 117.8 all-gather.6
  130.7 40.6 all-gather.8
  735.2 92.0 all-reduce.10
  829.3 60.6 all-gather.10
  891.9 59.0 all-gather.12
  952.9 59.0 all-gather.14
  1027.6 92.6 all-reduce.14
  1122.6 55.7 all-reduce.12
  1688.2 94.0 all-reduce.16
  1786.1 130.1 reduce-scatter.18
  1920.3 162.1 reduce-scatter.8
  2086.9 68.0 reduce-scatter.10
  2159.5 116.9 reduce-scatter.12
  2280.9 117.0 reduce-scatter.14
  2402.4 117.0 reduce-scatter.16
where the time goes:
time: 2550 us; the launch traced here: 2530 us
  waiting for transfers between devices  1100 us (43%)
  matrix products  573 us (22%)
  local copies, waits for them, and re-layouts  387 us (15%)
  other arithmetic  255 us (10%)
  blocking collectives  152 us (6%)
  loops' own time  27.4 us (1%)
    another operation x6, other arithmetic, householder_attention(): jax.scipy.linalg.solve_triangular(system, right_side, lower=True, unit_di...  178 us
    reduce_scatter x1, waiting for transfers between devices, body(): lax.psum_scatter(grad_in, ('dp', 'wid'), scatter_dimension=0, tiled=True)  127 us
    unnamed x2, blocking collectives  125 us
    reduce_scatter x1, waiting for transfers between devices, body(): lax.psum_scatter(grad_gate, ('dp', 'wid'), scatter_dimension=0, tiled=True)  122 us
    reduce_scatter x1, waiting for transfers between devices, body(): lax.psum_scatter(grad_down, ('dp', 'wid'), scatter_dimension=1, tiled=True)  122 us
    reduce_scatter x1, waiting for transfers between devices, body(): lax.psum_scatter(grad_up, ('dp', 'wid'), scatter_dimension=0, tiled=True)  122 us
    unnamed x16, waiting for transfers between devices  119 us
    dot_general x48, matrix products, sweep_step(): jnp.einsum('ihd,jhd->hij', moved_rows, keys_here, precision=highest)  107 us
  transfers between devices with their start and end apart: 19, of which 14 were waited for; matrix products, arithmetic and copies ran while one was open for 26% of the time, Pallas kernels for 0%

commit v1 on v0

--- a/solution.py
+++ b/solution.py
@@ -183,7 +183,7 @@
     )
     grad_gate = jnp.einsum("td,tf->df", mixed, grad_gate_pre, preferred_element_type=jnp.float32)
     grad_up = jnp.einsum("td,tf->df", mixed, grad_up_pre, preferred_element_type=jnp.float32)
-    grad_mixed = lax.psum(grad_mixed_part, "hid")
+    grad_mixed = jnp.sum(lax.all_gather(grad_mixed_part, "hid"), axis=0)
     grad_gain_two, grad_middle = norm_back(middle, scale_two, gain_two, grad_mixed)
     grad_middle = grad_middle + token_grad.astype(jnp.float32)
     grad_branch = grad_middle.astype(jnp.bfloat16)

time: 2550 us -> 2580 us (1.012)
    all_gather x0 -> x1, waiting for transfers between devices: none -> 102 us  [body(): grad_mixed = jnp.sum(lax.all_gather(grad_mixed_part, 'hid'), axis=0)]
    psum x1 -> x0, waiting for transfers between devices: 78.6 us -> none  [body(): grad_mixed = lax.psum(grad_mixed_part, 'hid')]
  transfers between devices with their start and end apart: 19 -> 19, of which waited for: 14 -> 14; matrix products, arithmetic and copies ran while one was open for 26% -> 27% of each run, Pallas kernels for 0% -> 0%
where the time goes in v1:
time: 2580 us; the launch traced here: 2560 us
  waiting for transfers between devices  1110 us (43%)
  matrix products  572 us (22%)
  local copies, waits for them, and re-layouts  387 us (15%)
  other arithmetic  267 us (10%)
  blocking collectives  153 us (6%)
  loops' own time  27.4 us (1%)
    another operation x6, other arithmetic, householder_attention(): jax.scipy.linalg.solve_triangular(system, right_side, lower=True, unit_di...  178 us
    reduce_scatter x1, waiting for transfers between devices, body(): lax.psum_scatter(grad_in, ('dp', 'wid'), scatter_dimension=0, tiled=True)  127 us
    unnamed x2, blocking collectives  125 us
    reduce_scatter x1, waiting for transfers between devices, body(): lax.psum_scatter(grad_up, ('dp', 'wid'), scatter_dimension=0, tiled=True)  122 us
    reduce_scatter x1, waiting for transfers between devices, body(): lax.psum_scatter(grad_down, ('dp', 'wid'), scatter_dimension=1, tiled=True)  122 us
    reduce_scatter x1, waiting for transfers between devices, body(): lax.psum_scatter(grad_gate, ('dp', 'wid'), scatter_dimension=0, tiled=True)  118 us
    unnamed x16, waiting for transfers between devices  113 us
    dot_general x48, matrix products, sweep_step(): jnp.einsum('ihd,jhd->hij', moved_rows, keys_here, precision=highest)  107 us
  transfers between devices with their start and end apart: 19, of which 14 were waited for; matrix products, arithmetic and copies ran while one was open for 27% of the time, Pallas kernels for 0%

profile of v1, /device:TPU:0, one launch (start us, length us, event | category | flops | bytes accessed | tf_op | source)
XLA Modules:
  0.0 2558.2 jit_solution(9289017855896606336)
XLA Ops:
  9.3 6.5 all-to-all-start
  18.3 89.2 %all-reduce.5 = (bf16[1536]{0:T(1024)(128)(2,1)S(1)}, bf16[1536]{0:T(1024)(128)(2,1)S(1)}) all-reduce(bf16[1536]{0:T(1024)(128)(2,1)S(1)} %dynamic-update-slice, bf16[1536]{0:T(1024)(128)(2,1)S(1)} %dynamic-update-slice.1), channel_id=1, replica_groups=mesh['dp'=2,'hid'=4,'wid'=4] {'dp','wid'}, use_global_device_ids=true, to_apply=%add | all-reduce | flops 3072 | bytes 12288
  107.6 27.1 %all-gather.1 = bf16[8,192,3]{1,2,0:T(4,128)(2,1)S(1)} all-gather(bf16[1,192,3]{1,2,0:T(4,128)(2,1)S(1)} %bitcast.622), channel_id=1, replica_groups=mesh['dp'=2,'hid'=4,'wid'=4] {'dp','wid'}, dimensions={0}, use_global_device_ids=true | all-gather | bytes 10368 | tf_op jit(solution)/shard_map/all_gather | solution.py:120
  142.8 6.2 fusion.66
  158.3 177.1 %custom-call.8 = f32[12,3,1,64,64]{3,4,2,1,0:T(8,128)S(1)} custom-call(f32[12,3,1,64,64]{4,3,2,1,0:T(8,128)S(1)} %add_bitcast_fusion), custom_call_target="InvertDiagBlocksLowerTriangular" | custom-call | tf_op jit(solution)/shard_map/jit(_solve_triangular)/vmap(vmap())/triangular_solve/custom-call.1 | solution.py:29
  360.9 4.6 fusion.82
  372.6 6.7 broadcast_in_dim.127
  379.3 3.6 broadcast.244.clone.1
  383.0 167.9 %while.59 = (s32[]{:T(128)}, f32[768,3,128]{0,2,1:T(8,128)S(1)}, f32[12,3,768,64]{2,3,1,0:T(8,128)}, f32[12,768,3,128]{1,3,2,0:T(8,128)}, f32[12,64,3,128]{3,1,2...) while((s32[]{:T(128)}, f32[768,3,128]{0,2,1:T(8,128)S(1)}, ...), condition=%wide.region_12.14_spmd.clone, body=%wide.region_11.13_spmd.sunk.clone | while | flops 793018368 | bytes 12189915 | solution.py:76
  550.9 3.7 broadcast.244.clone
  554.7 154.9 %while.58 = (s32[]{:T(128)}, f32[768,3,128]{0,2,1:T(8,128)S(1)}, f32[12,3,768,64]{2,3,1,0:T(8,128)}, f32[12,64,3,128]{3,1,2,0:T(8,128)}, f32[12,3,64,64]{2,3,1,0...) while((s32[]{:T(128)}, f32[768,3,128]{0,2,1:T(8,128)S(1)}, ...), condition=%wide.region_3.5_spmd.clone, body=%wide.region_2.4_spmd.sunk.clone | while | flops 793018368 | bytes 9830607 | solution.py:76
  709.6 6.3 select_reduce_fusion.1
  718.8 3.9 exponential_reduce_fusion
  726.1 3.7 convolution_convert_fusion.1
  729.8 5.1 fusion.167
  736.2 3.8 all-to-all-start.2
  740.6 39.9 %all-to-all-done.2 = bf16[4,768,384]{2,1,0:T(8,128)(2,1)S(1)} async-done(((bf16[4,768,384]{2,1,0:T(8,128)(2,1)}), bf16[4,768,384]{2,1,0:T(8,128)(2,1)S(1)}, u32[]{:S(2)}, u32[]{:S(2)}) %all-to-all-start.2) | async-done | bytes 2359328 | tf_op jit(solution)/shard_map/all_to_all | solution.py:114
  783.8 43.4 %all-reduce.10.cloned.1.call-done = f32[768,1536]{1,0:T(8,128)} async-done(((f32[768,1536]{1,0:T(8,128)}), f32[768,1536]{1,0:T(8,128)}) %all-reduce.10.cloned.1.call-update) | async-done | bytes 4718608 | tf_op jit(solution)/shard_map/psum | solution.py:154
  827.2 4.4 multiply_reduce_fusion.5
  835.6 54.2 %all-gather.13.cloned.1.call-done = bf16[1536,1024]{1,0:T(8,128)(2,1)} async-done(((bf16[192,1024]{1,0:T(8,128)(2,1)}), bf16[1536,1024]{1,0:T(8,128)(2,1)}) %all-gather.13.cloned.1.call-update) | async-done | bytes 3145744 | tf_op jit(solution)/shard_map/all_gather | solution.py:122
  889.8 6.8 fusion.168
  896.7 54.2 %all-gather.15.cloned.1.call-done = bf16[1536,1024]{1,0:T(8,128)(2,1)} async-done(((bf16[192,1024]{1,0:T(8,128)(2,1)}), bf16[1536,1024]{1,0:T(8,128)(2,1)}) %all-gather.15.cloned.1.call-update) | async-done | bytes 3145744 | tf_op jit(solution)/shard_map/all_gather | solution.py:123
  950.9 6.8 fusion.169
  957.7 54.2 %all-gather.17.cloned.1.call-done = bf16[1024,1536]{0,1:T(8,128)(2,1)} async-done(((bf16[1024,192]{0,1:T(8,128)(2,1)}), bf16[1024,1536]{0,1:T(8,128)(2,1)}) %all-gather.17.cloned.1.call-update) | async-done | bytes 3145744 | tf_op jit(solution)/shard_map/all_gather | solution.py:124
  1011.9 7.9 multiply_convert_fusion.2
  1022.9 4.4 convolution_add_fusion
  1028.7 5.8 convolution_convert_fusion
  1034.5 5.0 multiply_bitcast_fusion
  1039.5 5.0 copy.201
  1044.6 101.6 %all-gather.19.cloned.1.call-done = f32[3072,1536]{1,0:T(8,128)} async-done(((f32[768,1536]{1,0:T(8,128)}), f32[3072,1536]{1,0:T(8,128)}) %all-gather.19.cloned.1.call-update) | async-done | bytes 18874384 | tf_op jit(solution)/shard_map/all_gather | solution.py:186
  1146.1 11.3 reduce_sum.147
  1157.4 5.8 multiply_reduce_fusion.1
  1163.2 41.0 %all-reduce.12.cloned.1.call-done = bf16[768,1536]{1,0:T(8,128)(2,1)} async-done(((bf16[768,1536]{1,0:T(8,128)(2,1)}), bf16[768,1536]{1,0:T(8,128)(2,1)}) %all-reduce.12.cloned.1.call-update) | async-done | bytes 2359312 | tf_op jit(solution)/shard_map/psum | solution.py:163
  1204.2 7.9 convert_add_fusion
  1214.3 9.0 subtract_exponential_fusion
  1225.9 3.5 select_multiply_fusion
  1229.4 3.7 copy.346
  1233.1 388.5 %while.60 = (s32[]{:T(128)}, f32[768,3,128]{2,0,1:T(8,128)}, f32[12,64,3,128]{3,1,2,0:T(8,128)}, f32[12,64,3,128]{3,1,2,0:T(8,128)}, f32[12,3,64,64]{3,2,1,0:T(8...) while((s32[]{:T(128)}, f32[768,3,128]{2,0,1:T(8,128)}, ...), condition=%wide.region_19.21_spmd.clone.clone, body=%wide.region_18.20_spmd.clone.sunk.clone | while | flops 1926684672 | bytes 39472068 | solution.py:76
  1629.0 3.4 convolution_add_fusion.3
  1635.7 3.5 convolution_add_fusion.2
  1654.6 3.5 fusion.75
  1676.3 10.9 fusion.86
  1689.5 3.8 fusion.81
  1703.2 5.9 fusion.125
  1709.1 4.5 bitcast_add_fusion
  1715.3 4.1 fusion.140
  1719.5 7.8 fusion.60
  1728.9 6.0 fusion.173
  1734.9 6.0 fusion.174
  1742.7 6.2 fusion.175
  1752.2 4.7 all-to-all-start.1
  1756.9 51.0 %all-reduce.14.cloned.1.call-done = f32[768,1536]{1,0:T(8,128)} async-done(((f32[768,1536]{1,0:T(8,128)}), f32[768,1536]{1,0:T(8,128)}) %all-reduce.14.cloned.1.call-update) | async-done | bytes 4718608 | tf_op jit(solution)/shard_map/psum | solution.py:208
  1807.9 5.1 multiply_reduce_fusion.2
  1813.0 4.5 subtract_add_fusion
  1819.9 5.1 all-to-all-start.3
  1825.1 5.2 fusion.103
  1830.9 110.9 %reduce-scatter.19.cloned.1.call-done = f32[192,3]{1,0:T(8,128)} async-done(((f32[1536,3]{1,0:T(8,128)}), f32[192,3]{1,0:T(8,128)}) %reduce-scatter.19.cloned.1.call-update) | async-done | bytes 2320
  1943.4 36.2 %all-reduce.4 = (f32[1536]{0:T(1024)S(1)}, f32[1536]{0:T(1024)S(1)}) all-reduce(f32[1536]{0:T(1024)S(1)} %get-tuple-element.653, f32[1536]{0:T(1024)S(1)} %copy-done.83), channel_id=3, replica_groups=mesh['dp'=2,'hid'=4,'wid'=4] {'dp','wid'}, use_global_device_ids=true, to_apply=%region_26.29.clone | all-reduce | flops 3072 | bytes 24576
  1980.9 127.2 %reduce-scatter.9.cloned.1.call-done = f32[192,4,384]{2,0,1:T(8,128)} async-done(((f32[1536,4,384]{2,0,1:T(8,128)}), f32[192,4,384]{2,0,1:T(8,128)}) %reduce-scatter.9.cloned.1.call-update) | async-done | bytes 1179664 | tf_op jit(solution)/shard_map/reduce_scatter | solution.py:215
  2111.1 118.4 %reduce-scatter.13.cloned.1.call-done = f32[192,1024]{1,0:T(8,128)} async-done(((f32[1536,1024]{1,0:T(8,128)}), f32[192,1024]{1,0:T(8,128)}) %reduce-scatter.13.cloned.1.call-update) | async-done | bytes 786448 | tf_op jit(solution)/shard_map/reduce_scatter | solution.py:218
  2229.5 121.7 %reduce-scatter.15.cloned.1.call-done = f32[192,1024]{1,0:T(8,128)} async-done(((f32[1536,1024]{1,0:T(8,128)}), f32[192,1024]{1,0:T(8,128)}) %reduce-scatter.15.cloned.1.call-update) | async-done | bytes 786448 | tf_op jit(solution)/shard_map/reduce_scatter | solution.py:219
  2351.2 121.6 %reduce-scatter.17.cloned.1.call-done = f32[1024,192]{0,1:T(8,128)} async-done(((f32[1024,1536]{0,1:T(8,128)}), f32[1024,192]{0,1:T(8,128)}) %reduce-scatter.17.cloned.1.call-update) | async-done | bytes 786448 | tf_op jit(solution)/shard_map/reduce_scatter | solution.py:220
  2472.8 72.4 %reduce-scatter.11.cloned.1.call-done = f32[384,192]{0,1:T(8,128)} async-done(((f32[384,1536]{0,1:T(8,128)}), f32[384,192]{0,1:T(8,128)}) %reduce-scatter.11.cloned.1.call-update) | async-done | bytes 294928 | tf_op jit(solution)/shard_map/reduce_scatter | solution.py:217
  2546.6 4.8 copy.420
  (1044 shorter events, 836.4 us)
Async XLA Ops:
  7.2 135.6 %all-gather.9.cloned.1.call-start = ((), (), s32[]{:S(2)}) async-start(), calls=%async_computation.10 | async-start | bytes 5308416 | tf_op jit(solution)/shard_map/all_gather | solution.py:119
  9.2 7.3 copy-start.87
  9.2 8.6 copy-start.90
  9.2 8.8 copy-start.91
  9.2 98.3 %copy-start.86 = (bf16[192,3]{0,1:T(4,128)(2,1)S(1)}, bf16[192,3]{0,1:T(4,128)(2,1)}, u32[]{:S(2)}) copy-start(bf16[192,3]{0,1:T(4,128)(2,1)} %param.27) | copy-start | bytes 3460
  9.2 125.5 %copy-start.85 = (s32[1,768]{1,0:T(1,128)S(1)}, s32[1,768]{1,0:T(1,128)}, u32[]{:S(2)}) copy-start(s32[1,768]{1,0:T(1,128)} %param.23) | copy-start | bytes 9220
  9.3 128.9 %all-to-all-start = ((bf16[4,768,384]{2,1,0:T(8,128)(2,1)}), bf16[4,768,384]{2,1,0:T(8,128)(2,1)S(1)}, u32[]{:S(2)}, u32[]{:S(2)}) async-start(bf16[4,768,384]{2,1,0:T(8,128)(2,1)} %bitcast.614), calls=%async_computation | async-start | bytes 4718592 | tf_op jit(solution)/shard_map/all_to_all | solution.py:113
  15.7 714.1 %all-gather.11.cloned.1.call-start = ((), (), s32[]{:S(2)}) async-start(), calls=%async_computation.11 | async-start | bytes 1327104 | tf_op jit(solution)/shard_map/all_gather | solution.py:121
  16.5 810.8 %all-reduce.10.cloned.1.call-start = ((), (), s32[]{:S(2)}) async-start(), calls=%async_computation.12 | async-start | bytes 9437184 | tf_op jit(solution)/shard_map/psum | solution.py:154
  107.6 33.1 %copy-start.69 = (f32[1536]{0:T(1024)}, f32[1536]{0:T(1024)S(1)}, u32[]{:S(2)}) copy-start(f32[1536]{0:T(1024)S(1)} %convert_element_type.109) | copy-start | bytes 18436
  134.8 6.4 copy-start.72
  135.5 22.2 copy-start.58
  135.6 22.1 copy-start.65
  135.6 22.1 copy-start.79
  142.8 14.9 copy-start.61
  154.6 213.7 %copy-start = (f32[12,64,3,128]{3,1,0,2:T(8,128)}, f32[12,64,3,128]{3,1,0,2:T(8,128)S(1)}, u32[]{:S(2)}) copy-start(f32[12,64,3,128]{3,1,0,2:T(8,128)S(1)} %broadcast_multiply_fusion) | copy-start | bytes 3538948
  338.6 13.3 copy-start.10
  346.5 14.3 copy-start.14
  554.7 154.9 %copy-start.50 = (pred[768,12,64]{0,2,1:T(8,128)(4,1)S(1)}, pred[768,12,64]{0,2,1:T(8,128)(4,1)}, u32[]{:S(2)}) copy-start(pred[768,12,64]{0,2,1:T(8,128)(4,1)} %fusion.65) | copy-start | bytes 1769476
  709.6 6.4 slice-start.2
  709.6 7.2 slice-start.3
  709.6 9.2 copy-start.7
  729.8 5.2 copy-start.48
  735.0 154.8 %all-gather.13.cloned.1.call-start = ((), (), s32[]{:S(2)}) async-start(), calls=%async_computation.13 | async-start | bytes 3538944 | tf_op jit(solution)/shard_map/all_gather | solution.py:122
  735.6 215.3 %all-gather.15.cloned.1.call-start = ((), (), s32[]{:S(2)}) async-start(), calls=%async_computation.14 | async-start | bytes 3538944 | tf_op jit(solution)/shard_map/all_gather | solution.py:123
  736.2 44.3 %all-to-all-start.2 = ((bf16[4,768,384]{2,1,0:T(8,128)(2,1)}), bf16[4,768,384]{2,1,0:T(8,128)(2,1)S(1)}, u32[]{:S(2)}, u32[]{:S(2)}) async-start(bf16[4,768,384]{2,1,0:T(8,128)(2,1)} %bitcast.615), calls=%async_computation.2 | async-start | bytes 4718592 | tf_op jit(solution)/shard_map/all_to_all | solution.py:114
  739.9 272.0 %all-gather.17.cloned.1.call-start = ((), (), s32[]{:S(2)}) async-start(), calls=%async_computation.15 | async-start | bytes 3538944 | tf_op jit(solution)/shard_map/all_gather | solution.py:124
  740.5 405.6 %all-gather.19.cloned.1.call-start = ((), (), s32[]{:S(2)}) async-start(), calls=%async_computation.23 | async-start | bytes 23592960 | tf_op jit(solution)/shard_map/all_gather | solution.py:186
  783.8 228.1 %copy-start.44 = (bf16[4,96,8,384]{3,2,0,1:T(8,128)(2,1)}, bf16[4,96,8,384]{3,2,0,1:T(8,128)(2,1)S(1)}, u32[]{:S(2)}) copy-start(bf16[4,96,8,384]{3,2,0,1:T(8,128)(2,1)S(1)} %copy.301) | copy-start | bytes 7077892
  1011.9 7.9 copy-start.88
  1027.3 176.8 %all-reduce.12.cloned.1.call-start = ((), (), s32[]{:S(2)}) async-start(), calls=%async_computation.16 | async-start | bytes 4718592 | tf_op jit(solution)/shard_map/psum | solution.py:163
  1034.5 773.4 %all-reduce.14.cloned.1.call-start = ((), (), s32[]{:S(2)}) async-start(), calls=%async_computation.17 | async-start | bytes 9437184 | tf_op jit(solution)/shard_map/psum | solution.py:208
  1157.4 56.9 %slice-start = ((s8[7077888]{0:T(1024)(128)(4,1)}), s8[2883584]{0:T(1024)(128)(4,1)S(1)}, s32[]{:S(2)}) async-start(s8[7077888]{0:T(1024)(128)(4,1)} %bitcast.576), calls=%async_computation.25 | async-start | bytes 5767168
  1204.2 7.9 copy-start.56
  1204.2 10.1 slice-start.1
  1214.3 9.1 copy-start.51
  1233.1 388.5 %copy-start.1 = (f32[12,64,3,128]{3,1,0,2:T(8,128)S(1)}, f32[12,64,3,128]{3,1,0,2:T(8,128)}, u32[]{:S(2)}) copy-start(f32[12,64,3,128]{3,1,0,2:T(8,128)} %copy-done) | copy-start | bytes 3538948
  1310.0 3.7 copy-start.19
  1342.2 3.7 copy-start.19
  1374.8 3.7 copy-start.19
  1439.6 3.7 copy-start.19
  1471.9 3.7 copy-start.19
  1504.5 3.7 copy-start.19
  1569.3 3.7 copy-start.19
  1601.4 3.7 copy-start.19
  1672.1 4.2 copy-start.52
  1689.4 3.8 copy-start.41
  1703.2 5.9 copy-start.74
  1703.2 5.9 copy-start.71
  1703.2 5.9 copy-start.73
  1713.6 228.2 %reduce-scatter.19.cloned.1.call-start = ((), (), s32[]{:S(2)}) async-start(), calls=%async_computation.24 | async-start | bytes 884736
  1719.4 388.6 %reduce-scatter.9.cloned.1.call-start = ((), (), s32[]{:S(2)}) async-start(), calls=%async_computation.18 | async-start | bytes 10616832 | tf_op jit(solution)/shard_map/reduce_scatter | solution.py:215
  1727.2 502.3 %reduce-scatter.13.cloned.1.call-start = ((), (), s32[]{:S(2)}) async-start(), calls=%async_computation.20 | async-start | bytes 7077888 | tf_op jit(solution)/shard_map/reduce_scatter | solution.py:218
  1734.9 616.3 %reduce-scatter.15.cloned.1.call-start = ((), (), s32[]{:S(2)}) async-start(), calls=%async_computation.21 | async-start | bytes 7077888 | tf_op jit(solution)/shard_map/reduce_scatter | solution.py:219
  1741.0 731.8 %reduce-scatter.17.cloned.1.call-start = ((), (), s32[]{:S(2)}) async-start(), calls=%async_computation.22 | async-start | bytes 7077888 | tf_op jit(solution)/shard_map/reduce_scatter | solution.py:220
  1752.2 55.7 %copy-start.70 = (f32[1536]{0:T(1024)S(1)}, f32[1536]{0:T(1024)}, u32[]{:S(2)}) copy-start(f32[1536]{0:T(1024)} %copy-done.69) | copy-start | bytes 18436
  1752.2 55.7 %copy-start.82 = (f32[768]{0:T(1024)S(1)}, f32[768]{0:T(1024)}, u32[]{:S(2)}) copy-start(f32[768]{0:T(1024)} %copy-done.81) | copy-start | bytes 9220
  1752.2 67.8 %all-to-all-start.1 = ((bf16[768,4,384]{2,0,1:T(8,128)(2,1)}), bf16[768,4,384]{2,0,1:T(8,128)(2,1)S(1)}, u32[]{:S(2)}, u32[]{:S(2)}) async-start(bf16[768,4,384]{2,0,1:T(8,128)(2,1)} %bitcast.605), calls=%async_computation.1 | async-start | bytes 4718592 | tf_op jit(solution)/shard_map/all_to_all | solution.py:167
  1756.9 56.1 %copy-start.84 = (f32[768]{0:T(1024)S(1)}, f32[768]{0:T(1024)}, u32[]{:S(2)}) copy-start(f32[768]{0:T(1024)} %get-tuple-element.744) | copy-start | bytes 9220
  1807.9 5.1 copy-start.22
  1819.9 5.2 copy-start.49
  1819.9 160.9 %all-to-all-start.3 = ((f32[768,4,384]{2,0,1:T(8,128)}), f32[768,4,384]{2,0,1:T(8,128)}, u32[]{:S(2)}, u32[]{:S(2)}) async-start(f32[768,4,384]{2,0,1:T(8,128)} %bitcast.587), calls=%async_computation.3 | async-start | bytes 9437184 | tf_op jit(solution)/shard_map/all_to_all | solution.py:211
  1825.1 720.1 %reduce-scatter.11.cloned.1.call-start = ((), (), s32[]{:S(2)}) async-start(), calls=%async_computation.19 | async-start | bytes 2654208 | tf_op jit(solution)/shard_map/reduce_scatter | solution.py:217
  1830.3 113.0 %copy-start.83 = (f32[1536]{0:T(1024)S(1)}, f32[1536]{0:T(1024)}, u32[]{:S(2)}) copy-start(f32[1536]{0:T(1024)} %get-tuple-element.651) | copy-start | bytes 18436
  (142 other events, 298.4 us)
Sparse Core Ops, SparseCore 0:
  10.7 117.8 all-gather.8
  130.7 40.5 all-gather.10
  735.1 92.0 all-reduce.9
  829.2 60.6 all-gather.12
  891.8 59.0 all-gather.14
  952.8 59.0 all-gather.16
  1027.4 118.6 all-gather.18
  1148.5 55.6 all-reduce.11
  1713.7 94.0 all-reduce.13
  1811.6 130.1 reduce-scatter.18
  1945.8 162.1 reduce-scatter.8
  2112.5 116.9 reduce-scatter.12
  2234.1 117.0 reduce-scatter.14
  2355.6 117.0 reduce-scatter.16
  2477.1 68.0 reduce-scatter.10
